TPU v7x, 32 devices: a whole 2x2x4 slice. The times are simulated.
32 devices in a mesh: band: 4 (over y, core), ma: 8 (over z, x).
Axes of the slice: x: 2, y: 2, z: 4, core: 2. Of those that a mesh axis runs over, the one named last changes fastest.
Arguments:
- sky_maps: bfloat16 [64, 64, 2, 16384], P(None, ('band', 'ma')), may hold values from -6 to 6
- hi_cycles: int32 [64], P(('band', 'ma')), may hold values from 4096 to 8191, as said below
- lo_cycles: int32 [64], P(('band', 'ma')), may hold values from 1024 to 2047, as said below
- azimuth_orders: int32 [128], replicated, may hold values from 0 to 3071, as said below
- legendre_hi: bfloat16 [128, 3072, 64], P(('band', 'ma')), may hold values from -0.75 to 0.75
- legendre_lo: bfloat16 [128, 3072, 64], P(('band', 'ma')), may hold values from -0.109375 to 0.109375
- beam_weights: float32 [3072], replicated, may hold values from 0.05 to 1
Outputs:
- smoothed_maps: float32 [64, 64, 2, 4096], P(None, ('band', 'ma'))
Inputs may be any that keep to these rules, and one draw needn't show every extreme that they name: `hi_cycles`: distinct northern equatorial-belt cycles. `lo_cycles`: distinct northern equatorial-belt cycles. `azimuth_orders`: distinct orders.
All inputs are finite; a program needn't handle non-finite values.
Results may differ from a plain program's by a relative error of at most 0.0038.
Values may be sent and summed in bfloat16 or wider, within the bound.
No kernel may reach another device: no remote copies, remote signals or barrier semaphores. Data moves between devices by JAX's collectives and lax.ppermute only.
A program may use at most 192 MiB of HBM per device.

v0:
```python
import math
import jax
import jax.numpy as jnp
from jax import lax
from jax.sharding import PartitionSpec as P

NSIDE_HI = 4096
NSIDE_LO = 1024
LROWS = 3072
NPIX_HI = 16384
NPIX_LO = 4096
THREE_PASS = lax.Precision.HIGH


def angle_grid(first, second, length):
    product = first[:, None] * second[None, :] % length
    return product.astype(jnp.float32) * (2.0 * math.pi / length)


def cycle_offsets(cycle_ids, side_count):
    return ((cycle_ids - side_count + 1) % 2).astype(jnp.float32)


def per_device(
    sky_maps, hi_cycles, lo_cycles, azimuth_orders, legendre_hi, legendre_lo, beam_weights
):
    map_count = sky_maps.shape[0]
    pair_local = sky_maps.shape[1]
    select_total = azimuth_orders.shape[0]
    owned = legendre_hi.shape[0]
    half_cols = 2 * map_count
    pixels_hi = jnp.arange(NPIX_HI, dtype=jnp.int32)
    angles = angle_grid(pixels_hi, azimuth_orders, NPIX_HI)
    forward_table = jnp.concatenate([jnp.cos(angles), jnp.sin(angles)], axis=1).astype(jnp.bfloat16)
    raw_sums = jnp.dot(
        sky_maps.reshape(-1, NPIX_HI), forward_table, preferred_element_type=jnp.float32
    )
    raw_sums = raw_sums.reshape(map_count, pair_local, 2, 2, select_total)
    real_raw = raw_sums[:, :, :, 0]
    imag_raw = -raw_sums[:, :, :, 1]
    offsets_hi = cycle_offsets(hi_cycles, NSIDE_HI)
    theta_hi = math.pi * offsets_hi[:, None] * azimuth_orders.astype(jnp.float32)[None, :] / NPIX_HI
    cos_hi = jnp.cos(theta_hi)[None, :, None, :]
    sin_hi = jnp.sin(theta_hi)[None, :, None, :]
    scale_hi = 1.0 / math.sqrt(NPIX_HI)
    real_coef = (real_raw * cos_hi + imag_raw * sin_hi) * scale_hi
    imag_coef = (imag_raw * cos_hi - real_raw * sin_hi) * scale_hi
    stacked = jnp.stack([real_coef, imag_coef], axis=3)
    outgoing = (
        jnp.transpose(stacked, (4, 1, 2, 3, 0))
        .reshape(select_total, pair_local, 4 * map_count)
        .astype(jnp.bfloat16)
    )
    owner = lax.axis_index(("band", "ma"))
    own_orders = lax.dynamic_slice_in_dim(azimuth_orders, owner * owned, owned)
    degrees = jnp.arange(LROWS, dtype=jnp.int32)[None, :]
    parity = (degrees + own_orders[:, None]) % 2
    signs_lm = 1.0 - 2.0 * parity.astype(jnp.float32)
    beam_mask = jnp.where(degrees >= own_orders[:, None], beam_weights[None, :], 0.0)
    received = lax.all_to_all(outgoing, ("band", "ma"), split_axis=0, concat_axis=1, tiled=True)
    analysis = jnp.einsum("mlr,mrc->mlc", legendre_hi, received, preferred_element_type=jnp.float32)
    harmonic = analysis[:, :, :half_cols] + signs_lm[..., None] * analysis[:, :, half_cols:]
    weighted = beam_mask[..., None] * harmonic
    paired = jnp.concatenate([weighted, signs_lm[..., None] * weighted], axis=2)
    synthesized = jnp.einsum(
        "mlq,mlc->mqc",
        legendre_lo,
        paired,
        precision=THREE_PASS,
        preferred_element_type=jnp.float32,
    )
    returned = lax.all_to_all(synthesized, ("band", "ma"), split_axis=1, concat_axis=0, tiled=True)
    low_local = returned.shape[1]
    parts_low = returned.reshape(select_total, low_local, 2, 2, map_count)
    real_low = parts_low[:, :, :, 0]
    imag_low = parts_low[:, :, :, 1]
    offsets_lo = cycle_offsets(lo_cycles, NSIDE_LO)
    theta_lo = math.pi * azimuth_orders.astype(jnp.float32)[:, None] * offsets_lo[None, :] / NPIX_LO
    cos_lo = jnp.cos(theta_lo)[:, :, None, None]
    sin_lo = jnp.sin(theta_lo)[:, :, None, None]
    real_rot = real_low * cos_lo - imag_low * sin_lo
    imag_rot = imag_low * cos_lo + real_low * sin_lo
    spectra = jnp.stack([real_rot, imag_rot], axis=0)
    spectra = jnp.transpose(spectra, (4, 2, 3, 0, 1)).reshape(-1, 2 * select_total)
    pixels_lo = jnp.arange(NPIX_LO, dtype=jnp.int32)
    angles_lo = angle_grid(azimuth_orders, pixels_lo, NPIX_LO)
    inverse_table = jnp.concatenate([jnp.cos(angles_lo), -jnp.sin(angles_lo)], axis=0)
    pixels_out = jnp.dot(
        spectra, inverse_table, precision=THREE_PASS, preferred_element_type=jnp.float32
    )
    pixels_out = pixels_out * math.sqrt(2.0 / select_total)
    return pixels_out.reshape(map_count, low_local, 2, NPIX_LO)


def solution(mesh):
    return jax.shard_map(
        per_device,
        mesh=mesh,
        in_specs=(
            P(None, ("band", "ma"), None, None),
            P(("band", "ma")),
            P(("band", "ma")),
            P(),
            P(("band", "ma"), None, None),
            P(("band", "ma"), None, None),
            P(),
        ),
        out_specs=P(None, ("band", "ma"), None, None),
        check_vma=False,
    )
```

profile of v0, /device:TPU:0, one launch (start us, length us, event | category | flops | bytes accessed | tf_op | source)
XLA Modules:
  0.0 116.5 jit_solution(8038480277856101105)
XLA Ops:
  0.0 35.4 %cosine_convert_fusion = (bf16[16384,128]{1,0:T(8,128)(2,1)}, bf16[16384,128]{1,0:T(8,128)(2,1)}) fusion(s32[128]{0:T(128)} %param.10), kind=kLoop, calls=%fused_computation.15 | loop fusion | flops 33554432 | bytes 8389120 | tf_op jit(solution)/shard_map/convert.2
  35.4 13.1 %reshape.236 = bf16[256,16384]{1,0:T(8,128)(2,1)} reshape(bf16[64,2,2,16384]{3,2,1,0:T(2,128)(2,1)} %param.7) | data formatting | bytes 16777216 | tf_op jit(solution)/shard_map/reshape | solution.py:36
  48.6 8.3 %fusion.25 = f32[256,256]{0,1:T(8,128)S(1)} fusion(bf16[256,16384]{1,0:T(8,128)(2,1)} %reshape.236, bf16[16384,128]{1,0:T(8,128)(2,1)} %get-tuple-element.22, bf16[16384,128]{1,0:T(8,128)(2,1)} %get-tuple-element.21), kind=kOutput, calls=%fused_computation.38 | convolution fusion | flops 2164260864 | bytes 17039360 | tf_op jit(solution)/shard_map/dot_general | solution.py:35
  57.0 0.1 reshape.237
  57.1 0.2 fusion.53
  57.6 0.8 copy.30
  58.3 7.3 %all-to-all-start = ((bf16[128,2,256]{2,1,0:T(2,128)(2,1)}), bf16[128,2,256]{2,1,0:T(2,128)(2,1)S(1)}, u32[]{:S(2)}, u32[]{:S(2)}) async-start(bf16[128,2,256]{2,1,0:T(2,128)(2,1)} %copy.30), calls=%async_computation | async-start | bytes 262144 | tf_op jit(solution)/shard_map/all_to_all | solution.py:60
  65.8 0.1 fusion.38
  66.3 7.2 %all-to-all-done = bf16[128,2,256]{2,1,0:T(2,128)(2,1)S(1)} async-done(((bf16[128,2,256]{2,1,0:T(2,128)(2,1)}), bf16[128,2,256]{2,1,0:T(2,128)(2,1)S(1)}, u32[]{:S(2)}, u32[]{:S(2)}) %all-to-all-start) | async-done | bytes 131104 | tf_op jit(solution)/shard_map/all_to_all | solution.py:60
  73.7 1.8 %convolution_bitcast_fusion = f32[4,3072,256]{1,2,0:T(8,128)S(1)} fusion(bf16[4,64,256]{2,1,0:T(8,128)(2,1)S(1)} %all_to_all.27, bf16[4,3072,64]{1,2,0:T(8,128)(2,1)S(1)} %copy-done), kind=kOutput, calls=%fused_computation.19 | convolution fusion | flops 402653184 | bytes 14286848 | tf_op jit(solution)/shard_map/mlr,mrc->mlc/dot_general | solution.py:61
  75.5 5.6 %broadcast_multiply_fusion = (f32[4,3072,128]{1,2,0:T(8,128)}, f32[4,3072,128]{1,2,0:T(8,128)}) fusion(f32[4,3072]{1,0:T(4,128)S(1)} %get-tuple-element.20, f32[4,3072,256]{1,2,0:T(8,128)S(1)} %convolution_bitcast_fusion, f32[4,3072]{1,0:T(4,128)S(1)} %get-tuple-element.19), kind=kLoop, calls=%fused_computation.30 | loop fusion | flops 6291456 | bytes 25264128 | tf_op jit(solution)/shard_map/mul | solution.py:64
  81.1 6.9 %fusion.28 = f32[4,64,256]{2,1,0:T(8,128)S(1)} fusion(bf16[4,3072,64]{1,2,0:T(8,128)(2,1)S(1)} %copy-done.2, f32[4,3072,128]{1,2,0:T(8,128)} %get-tuple-element.5, f32[4,3072,128]{1,2,0:T(8,128)} %get-tuple-element.6), kind=kOutput, calls=%fused_computation.39 | convolution fusion | flops 1211105280 | bytes 14417920 | tf_op jit(solution)/shard_map/mlq,mlc->mqc/dot_general | solution.py:65
  88.0 0.9 copy.33
  88.9 2.8 %all-to-all-start.1 = ((f32[4,64,256]{2,0,1:T(4,128)}), f32[4,64,256]{2,0,1:T(4,128)S(1)}, u32[]{:S(2)}, u32[]{:S(2)}) async-start(f32[4,64,256]{2,0,1:T(4,128)} %copy.33), calls=%async_computation.1 | async-start | bytes 524288 | tf_op jit(solution)/shard_map/all_to_all | solution.py:72
  91.7 9.8 %fusion.31 = (f32[128,4096]{1,0:T(8,128)}, f32[128,4096]{1,0:T(8,128)}) fusion(s32[128]{0:T(128)S(1)} %copy-done.4), kind=kLoop, calls=%fused_computation.40 | loop fusion | flops 7864320 | bytes 4194816 | tf_op jit(solution)/shard_map/cos | solution.py:87
  101.4 0.5 all-to-all-done.1
  101.9 0.1 copy.56
  102.1 0.5 reshape.238
  102.5 0.4 fusion.52
  102.9 0.7 multiply_subtract_fusion
  103.7 0.3 maximum_bitcast_fusion
  103.9 0.4 copy.38
  104.3 6.3 %convolution_multiply_fusion = f32[256,4096]{1,0:T(8,128)} fusion(f32[128,4096]{1,0:T(8,128)} %get-tuple-element.24, f32[128,4096]{1,0:T(8,128)} %get-tuple-element.23, f32[32,8,2,128]{3,2,1,0:T(2,128)S(1)} %bitcast.31), kind=kOutput, calls=%fused_computation.23 | convolution fusion | flops 1612709888 | bytes 8650752 | tf_op jit(solution)/shard_map/dot_general | solution.py:88
  110.6 5.8 %reshape.240 = f32[64,2,2,4096]{3,2,1,0:T(2,128)} reshape(f32[256,4096]{1,0:T(8,128)} %convolution_multiply_fusion) | data formatting | bytes 8388608 | tf_op jit(solution)/shard_map/reshape | solution.py:92
  (28 shorter events, 0.9 us)
Async XLA Ops:
  0.0 73.6 %copy-start = (bf16[4,3072,64]{1,2,0:T(8,128)(2,1)S(1)}, bf16[4,3072,64]{1,2,0:T(8,128)(2,1)}, u32[]{:S(2)}) copy-start(bf16[4,3072,64]{1,2,0:T(8,128)(2,1)} %param.11) | copy-start | bytes 4718596
  0.0 35.4 %copy-start.4 = (s32[128]{0:T(128)S(1)}, s32[128]{0:T(128)}, u32[]{:S(2)}) copy-start(s32[128]{0:T(128)} %param.10) | copy-start | bytes 1540
  48.6 8.8 %copy-start.5 = (s32[2]{0:T(128)S(1)}, s32[2]{0:T(128)}, u32[]{:S(2)}) copy-start(s32[2]{0:T(128)} %param.8) | copy-start | bytes 28
  48.6 17.2 %copy-start.3 = (f32[3072]{0:T(1024)S(1)}, f32[3072]{0:T(1024)}, u32[]{:S(2)}) copy-start(f32[3072]{0:T(1024)} %param.13) | copy-start | bytes 36868
  48.6 17.4 %copy-start.6 = (s32[2]{0:T(128)S(1)}, s32[2]{0:T(128)}, u32[]{:S(2)}) copy-start(s32[2]{0:T(128)} %param.9) | copy-start | bytes 28
  58.3 15.1 %all-to-all-start = ((bf16[128,2,256]{2,1,0:T(2,128)(2,1)}), bf16[128,2,256]{2,1,0:T(2,128)(2,1)S(1)}, u32[]{:S(2)}, u32[]{:S(2)}) async-start(bf16[128,2,256]{2,1,0:T(2,128)(2,1)} %copy.30), calls=%async_computation | async-start | bytes 262144 | tf_op jit(solution)/shard_map/all_to_all | solution.py:60
  75.5 5.6 %copy-start.2 = (bf16[4,3072,64]{1,2,0:T(8,128)(2,1)S(1)}, bf16[4,3072,64]{1,2,0:T(8,128)(2,1)}, u32[]{:S(2)}) copy-start(bf16[4,3072,64]{1,2,0:T(8,128)(2,1)} %param.12) | copy-start | bytes 4718596
  88.9 13.0 %all-to-all-start.1 = ((f32[4,64,256]{2,0,1:T(4,128)}), f32[4,64,256]{2,0,1:T(4,128)S(1)}, u32[]{:S(2)}, u32[]{:S(2)}) async-start(f32[4,64,256]{2,0,1:T(4,128)} %copy.33), calls=%async_computation.1 | async-start | bytes 524288 | tf_op jit(solution)/shard_map/all_to_all | solution.py:72
  104.3 12.2 %copy-start.1 = (bf16[4,3072,64]{1,2,0:T(8,128)(2,1)S(1)}, bf16[4,3072,64]{1,2,0:T(8,128)(2,1)}, u32[]{:S(2)}) copy-start(bf16[4,3072,64]{1,2,0:T(8,128)(2,1)} %param.11) | copy-start | bytes 4718596
where the time goes:
time: 117 us; the launch traced here: 116 us
  other arithmetic  52.2 us (45%)
  matrix products  23.4 us (20%)
  local copies, waits for them, and re-layouts  22.9 us (20%)
  starting transfers between devices  10.1 us (9%)
  waiting for transfers between devices  7.68 us (7%)
    another operation x2, other arithmetic  35.5 us
    reshape x1, local copies, waits for them, and re-layouts, per_device(): sky_maps.reshape(-1, NPIX_HI)  13.1 us
    cos x1, other arithmetic, per_device(): jnp.cos(angles_lo)  9.79 us
    dot_general x1, matrix products, per_device(): jnp.dot(sky_maps.reshape(-1, NPIX_HI), forward_table, preferred_element_t...  8.27 us
    all_to_all x1, starting transfers between devices, per_device(): lax.all_to_all(outgoing, ('band', 'ma'), split_axis=0, concat_axis=1, til...  7.32 us
    all_to_all x1, waiting for transfers between devices, per_device(): lax.all_to_all(outgoing, ('band', 'ma'), split_axis=0, concat_axis=1, til...  7.21 us
    dot_general x1, matrix products, per_device(): jnp.einsum('mlq,mlc->mqc', legendre_lo, paired, precision=THREE_PASS, pre...  6.94 us
    dot_general x1, matrix products, per_device(): jnp.dot(spectra, inverse_table, precision=THREE_PASS, preferred_element_t...  6.33 us
  transfers between devices with their start and end apart: 2, of which 2 were waited for; matrix products, arithmetic and copies ran while one was open for 9% of the time, Pallas kernels for 0%

commit v1 on v0

--- a/solution.py
+++ b/solution.py
@@ -57,7 +57,15 @@
     parity = (degrees + own_orders[:, None]) % 2
     signs_lm = 1.0 - 2.0 * parity.astype(jnp.float32)
     beam_mask = jnp.where(degrees >= own_orders[:, None], beam_weights[None, :], 0.0)
-    received = lax.all_to_all(outgoing, ("band", "ma"), split_axis=0, concat_axis=1, tiled=True)
+    received = jnp.concatenate(
+        lax.all_to_all(
+            jnp.stack(jnp.split(outgoing, lax.axis_size(("band", "ma")), axis=0)),
+            ("band", "ma"),
+            0,
+            0,
+        ),
+        axis=1,
+    )
     analysis = jnp.einsum("mlr,mrc->mlc", legendre_hi, received, preferred_element_type=jnp.float32)
     harmonic = analysis[:, :, :half_cols] + signs_lm[..., None] * analysis[:, :, half_cols:]
     weighted = beam_mask[..., None] * harmonic

time: 117 us -> 175 us (1.50)
  local copies, waits for them, and re-layouts: 22.9 us -> 80.4 us
  waiting for transfers between devices: 7.68 us -> 5.05 us
  other arithmetic: 52.2 us -> 54.2 us
    unnamed x14 -> x43, local copies, waits for them, and re-layouts: 0.03 us -> 27.3 us
    another operation x0 -> x33, local copies, waits for them, and re-layouts: none -> 27.1 us  [per_device(): jnp.stack(jnp.split(outgoing, lax.axis_size(('band', 'ma')), axis=0))]
    split x0 -> x2, local copies, waits for them, and re-layouts: none -> 3.18 us  [per_device(): jnp.split(outgoing, lax.axis_size(('band', 'ma')), axis=0)]
    all_to_all x1, waiting for transfers between devices: 7.21 us -> 4.39 us  [per_device(): lax.all_to_all(jnp.stack(jnp.split(outgoing, lax.axis_size(('band', 'ma')...]
    another operation x3 -> x2, other arithmetic: 35.5 us -> 35.5 us
  transfers between devices with their start and end apart: 2 -> 2, of which waited for: 2 -> 2; matrix products, arithmetic and copies ran while one was open for 9% -> 8% of each run, Pallas kernels for 0% -> 0%
where the time goes in v1:
time: 175 us; the launch traced here: 173 us
  local copies, waits for them, and re-layouts  80.4 us (46%)
  other arithmetic  54.2 us (31%)
  matrix products  23.3 us (13%)
  starting transfers between devices  10.1 us (6%)
  waiting for transfers between devices  5.05 us (3%)
    another operation x2, other arithmetic  35.5 us
    unnamed x43, local copies, waits for them, and re-layouts  27.3 us
    another operation x33, local copies, waits for them, and re-layouts, per_device(): jnp.stack(jnp.split(outgoing, lax.axis_size(('band', 'ma')), axis=0))  27.1 us
    reshape x1, local copies, waits for them, and re-layouts, per_device(): sky_maps.reshape(-1, NPIX_HI)  13.1 us
    cos x1, other arithmetic, per_device(): jnp.cos(angles_lo)  9.77 us
    dot_general x1, matrix products, per_device(): jnp.dot(sky_maps.reshape(-1, NPIX_HI), forward_table, preferred_element_t...  8.25 us
    all_to_all x1, starting transfers between devices, per_device(): lax.all_to_all(jnp.stack(jnp.split(outgoing, lax.axis_size(('band', 'ma')...  7.51 us
    dot_general x1, matrix products, per_device(): jnp.einsum('mlq,mlc->mqc', legendre_lo, paired, precision=THREE_PASS, pre...  6.95 us
  transfers between devices with their start and end apart: 2, of which 2 were waited for; matrix products, arithmetic and copies ran while one was open for 8% of the time, Pallas kernels for 0%

profile of v1, /device:TPU:0, one launch (start us, length us, event | category | flops | bytes accessed | tf_op | source)
XLA Modules:
  0.0 173.2 jit_solution(471997547188920746)
XLA Ops:
  0.0 35.4 %cosine_convert_fusion = (bf16[16384,128]{1,0:T(8,128)(2,1)}, bf16[16384,128]{1,0:T(8,128)(2,1)}) fusion(s32[128]{0:T(128)} %param.10), kind=kLoop, calls=%fused_computation.15 | loop fusion | flops 33554432 | bytes 8389120 | tf_op jit(solution)/shard_map/convert.2
  35.4 13.1 %reshape.306 = bf16[256,16384]{1,0:T(8,128)(2,1)} reshape(bf16[64,2,2,16384]{3,2,1,0:T(2,128)(2,1)} %param.7) | data formatting | bytes 16777216 | tf_op jit(solution)/shard_map/reshape | solution.py:36
  48.6 8.2 %fusion.25 = f32[256,256]{0,1:T(8,128)S(1)} fusion(bf16[256,16384]{1,0:T(8,128)(2,1)} %reshape.306, bf16[16384,128]{1,0:T(8,128)(2,1)} %get-tuple-element.54, bf16[16384,128]{1,0:T(8,128)(2,1)} %get-tuple-element.53), kind=kOutput, calls=%fused_computation.38 | convolution fusion | flops 2164260864 | bytes 17039360 | tf_op jit(solution)/shard_map/dot_general | solution.py:35
  57.5 1.7 fusion.55
  63.9 1.6 copy.133
  65.5 1.6 copy.134
  67.1 1.6 copy.135
  70.3 1.6 copy.137
  71.9 1.6 copy.138
  73.5 1.6 copy.139
  75.1 1.6 copy.140
  76.7 1.6 copy.141
  78.3 1.6 copy.142
  79.9 1.6 copy.143
  81.5 1.6 copy.144
  115.2 7.5 %all-to-all-start = ((bf16[32,4,2,256]{3,2,1,0:T(2,128)(2,1)}), bf16[32,4,2,256]{3,2,1,0:T(2,128)(2,1)S(1)}, u32[]{:S(2)}, u32[]{:S(2)}) async-start(bf16[32,4,2,256]{3,2,1,0:T(2,128)(2,1)} %constant_dynamic-update-slice_fusion), calls=%async_computation | async-start | bytes 262144 | tf_op jit(solution)/shard_map/all_to_all | solution.py:61
  125.9 4.4 %all-to-all-done = bf16[32,4,2,256]{3,2,1,0:T(2,128)(2,1)S(1)} async-done(((bf16[32,4,2,256]{3,2,1,0:T(2,128)(2,1)}), bf16[32,4,2,256]{3,2,1,0:T(2,128)(2,1)S(1)}, u32[]{:S(2)}, u32[]{:S(2)}) %all-to-all-start) | async-done | bytes 131104 | tf_op jit(solution)/shard_map/all_to_all | solution.py:61
  130.5 1.8 %convolution_bitcast_fusion = f32[4,3072,256]{1,2,0:T(8,128)S(1)} fusion(bf16[4,64,256]{2,1,0:T(8,128)(2,1)S(1)} %reshape.309, bf16[4,3072,64]{1,2,0:T(8,128)(2,1)S(1)} %copy-done), kind=kOutput, calls=%fused_computation.19 | convolution fusion | flops 402653184 | bytes 14286848 | tf_op jit(solution)/shard_map/mlr,mrc->mlc/dot_general | solution.py:69
  132.3 5.5 %broadcast_multiply_fusion = (f32[4,3072,128]{1,2,0:T(8,128)}, f32[4,3072,128]{1,2,0:T(8,128)}) fusion(f32[4,3072]{1,0:T(4,128)S(1)} %get-tuple-element.52, f32[4,3072,256]{1,2,0:T(8,128)S(1)} %convolution_bitcast_fusion, f32[4,3072]{1,0:T(4,128)S(1)} %get-tuple-element.51), kind=kLoop, calls=%fused_computation.30 | loop fusion | flops 6291456 | bytes 25264128 | tf_op jit(solution)/shard_map/mul | solution.py:72
  137.8 7.0 %fusion.28 = f32[4,64,256]{2,1,0:T(8,128)S(1)} fusion(bf16[4,3072,64]{1,2,0:T(8,128)(2,1)S(1)} %copy-done.2, f32[4,3072,128]{1,2,0:T(8,128)} %get-tuple-element.5, f32[4,3072,128]{1,2,0:T(8,128)} %get-tuple-element.6), kind=kOutput, calls=%fused_computation.39 | convolution fusion | flops 1211105280 | bytes 14417920 | tf_op jit(solution)/shard_map/mlq,mlc->mqc/dot_general | solution.py:73
  145.7 2.6 %all-to-all-start.1 = ((f32[4,64,256]{2,0,1:T(4,128)}), f32[4,64,256]{2,0,1:T(4,128)S(1)}, u32[]{:S(2)}, u32[]{:S(2)}) async-start(f32[4,64,256]{2,0,1:T(4,128)} %copy.124), calls=%async_computation.1 | async-start | bytes 524288 | tf_op jit(solution)/shard_map/all_to_all | solution.py:80
  148.3 9.8 %fusion.31 = (f32[128,4096]{1,0:T(8,128)}, f32[128,4096]{1,0:T(8,128)}) fusion(s32[128]{0:T(128)S(1)} %copy-done.4), kind=kLoop, calls=%fused_computation.40 | loop fusion | flops 7864320 | bytes 4194816 | tf_op jit(solution)/shard_map/cos | solution.py:95
  161.1 6.3 %convolution_multiply_fusion = f32[256,4096]{1,0:T(8,128)} fusion(f32[128,4096]{1,0:T(8,128)} %get-tuple-element.56, f32[128,4096]{1,0:T(8,128)} %get-tuple-element.55, f32[32,8,2,128]{3,2,1,0:T(2,128)S(1)} %bitcast.60), kind=kOutput, calls=%fused_computation.23 | convolution fusion | flops 1612709888 | bytes 8650752 | tf_op jit(solution)/shard_map/dot_general | solution.py:96
  167.4 5.8 %reshape.312 = f32[64,2,2,4096]{3,2,1,0:T(2,128)} reshape(f32[256,4096]{1,0:T(8,128)} %convolution_multiply_fusion) | data formatting | bytes 8388608 | tf_op jit(solution)/shard_map/reshape | solution.py:100
  (91 shorter events, 46.3 us)
Async XLA Ops:
  0.0 130.5 %copy-start = (bf16[4,3072,64]{1,2,0:T(8,128)(2,1)S(1)}, bf16[4,3072,64]{1,2,0:T(8,128)(2,1)}, u32[]{:S(2)}) copy-start(bf16[4,3072,64]{1,2,0:T(8,128)(2,1)} %param.11) | copy-start | bytes 4718596
  0.0 35.4 %copy-start.3 = (s32[128]{0:T(128)S(1)}, s32[128]{0:T(128)}, u32[]{:S(2)}) copy-start(s32[128]{0:T(128)} %param.10) | copy-start | bytes 1540
  48.6 8.8 %copy-start.5 = (s32[2]{0:T(128)S(1)}, s32[2]{0:T(128)}, u32[]{:S(2)}) copy-start(s32[2]{0:T(128)} %param.8) | copy-start | bytes 28
  115.2 15.1 %all-to-all-start = ((bf16[32,4,2,256]{3,2,1,0:T(2,128)(2,1)}), bf16[32,4,2,256]{3,2,1,0:T(2,128)(2,1)S(1)}, u32[]{:S(2)}, u32[]{:S(2)}) async-start(bf16[32,4,2,256]{3,2,1,0:T(2,128)(2,1)} %constant_dynamic-update-slice_fusion), calls=%async_computation | async-start | bytes 262144 | tf_op jit(solution)/shard_map/all_to_all | solution.py:61
  132.3 5.5 %copy-start.2 = (bf16[4,3072,64]{1,2,0:T(8,128)(2,1)S(1)}, bf16[4,3072,64]{1,2,0:T(8,128)(2,1)}, u32[]{:S(2)}) copy-start(bf16[4,3072,64]{1,2,0:T(8,128)(2,1)} %param.12) | copy-start | bytes 4718596
  137.8 10.4 %copy-start.4 = (s32[128]{0:T(128)S(1)}, s32[128]{0:T(128)}, u32[]{:S(2)}) copy-start(s32[128]{0:T(128)} %param.10) | copy-start | bytes 1540
  145.7 13.0 %all-to-all-start.1 = ((f32[4,64,256]{2,0,1:T(4,128)}), f32[4,64,256]{2,0,1:T(4,128)S(1)}, u32[]{:S(2)}, u32[]{:S(2)}) async-start(f32[4,64,256]{2,0,1:T(4,128)} %copy.124), calls=%async_computation.1 | async-start | bytes 524288 | tf_op jit(solution)/shard_map/all_to_all | solution.py:80
  161.1 12.1 %copy-start.1 = (bf16[4,3072,64]{1,2,0:T(8,128)(2,1)S(1)}, bf16[4,3072,64]{1,2,0:T(8,128)(2,1)}, u32[]{:S(2)}) copy-start(bf16[4,3072,64]{1,2,0:T(8,128)(2,1)} %param.11) | copy-start | bytes 4718596
